TPU v7x, 256 devices: a whole 4x4x8 slice. The times are simulated.
256 devices in a mesh: net: 32 (over x, z), scen: 8 (over y, core).
Axes of the slice: x: 4, y: 4, z: 8, core: 2. Of those that a mesh axis runs over, the one named last changes fastest.
Arguments:
- arc_flows: float32 [256, 262144], P('scen', 'net'), may hold values from 0 to 1
- node_duals: float32 [256, 65536], P('scen', 'net'), may hold values from -6 to 6
- demand: float32 [256, 65536], P('scen', 'net'), may hold values from -6 to 6
- excess: float32 [256], P('scen'), may hold values from 0 to 0.5
- risk_duals: float32 [256], P('scen'), may hold values from 0.2 to 6
- threshold: float32 [1], replicated, may hold values from -2.5 to -1.5
- arc_costs: float32 [262144], P('net'), may hold values from 0.05 to 0.75
- local_blocks: bfloat16 [2048, 4, 128, 128], P('net'), may hold values from -0.125 to 0.125
- head_blocks: bfloat16 [2048, 128, 128], P('net'), may hold values from -0.125 to 0.125
- local_index: int32 [2048, 4], P('net'), may hold values from 0 to 15
- head_index: int32 [2048], P('net'), may hold values from 0 to 511, as said below
Outputs:
- flows_next: float32 [256, 262144], P('scen', 'net')
- duals_next: float32 [256, 65536], P('scen', 'net')
- excess_next: float32 [256], P('scen')
- risk_next: float32 [256], P('scen')
- threshold_next: float32 [1], replicated
Inputs may be any that keep to these rules, and one draw needn't show every extreme that they name: Among the arc blocks of one device, at most 4 have their head node block on any one device of net (head_index // 16 names the device), and in every device's arc blocks some device of net is named exactly 4 times.
All inputs are finite; a program needn't handle non-finite values.
Results may differ from a plain program's by a relative error of at most 0.0021.
Values may be sent and summed in bfloat16 or wider, within the bound.
A program may use at most 128 MiB of HBM per device.

v0:
```python
import jax
import jax.numpy as jnp
from jax import lax
from jax.sharding import PartitionSpec as P

ROUNDS = 3
primal_step = 0.5
dual_step = 0.5
risk_step = 1.0
tail_weight = 2.0


def per_device(
    arc_flows,
    node_duals,
    demand,
    excess,
    risk_duals,
    threshold,
    arc_costs,
    local_blocks,
    head_blocks,
    local_index,
    head_index,
):
    block_rows = local_blocks.shape[-1]
    scen_rows = arc_flows.shape[0]
    arc_blks = head_index.shape[0]
    node_blks = node_duals.shape[1] // block_rows
    touches = local_index.shape[1]
    net_size = lax.axis_size("net")
    scen_size = lax.axis_size("scen")
    slot_cap = max(2, (2 * arc_blks + net_size - 1) // net_size)
    slot_count = net_size * slot_cap
    arc_total = arc_flows.shape[1] * net_size
    scen_total = scen_rows * scen_size
    select_prec = lax.Precision.HIGH
    peer_dev = head_index // node_blks
    target = head_index % node_blks
    peer_hot = (peer_dev[:, None] == jnp.arange(net_size, dtype=jnp.int32)[None, :]).astype(
        jnp.int32
    )
    earlier = jnp.cumsum(peer_hot, axis=0) - peer_hot
    slot_rank = jnp.sum(earlier * peer_hot, axis=1)
    slot_ids = peer_dev * slot_cap + slot_rank
    slot_hot = slot_ids[:, None] == jnp.arange(slot_count, dtype=jnp.int32)[None, :]
    arc_ids = jnp.arange(arc_blks, dtype=jnp.int32)
    slot_arc = jnp.max(jnp.where(slot_hot, arc_ids[:, None], -1), axis=0)
    slot_filled = slot_arc >= 0
    slot_source = jnp.maximum(slot_arc, 0)
    wanted = jnp.max(jnp.where(slot_hot, target[:, None], -1), axis=0).reshape(net_size, slot_cap)
    asked = lax.all_to_all(wanted, "net", split_axis=0, concat_axis=0, tiled=True)
    asked_hot = asked.reshape(-1)[:, None] == jnp.arange(node_blks, dtype=jnp.int32)[None, :]
    local_hot = local_index[:, :, None] == jnp.arange(node_blks, dtype=jnp.int32)[None, None, :]
    asked_wide = asked_hot.astype(jnp.float32)
    local_wide = local_hot.astype(jnp.float32)
    local_half = local_hot.astype(jnp.bfloat16)
    flow_now = arc_flows
    dual_now = node_duals
    level = threshold
    excess_now = excess
    risk_now = risk_duals
    for iteration in range(ROUNDS):
        dual_panel = dual_now.astype(jnp.bfloat16)
        dual_grid = dual_panel.reshape(scen_rows, node_blks, block_rows)
        gathered = lax.all_gather(dual_panel, "net", axis=1, tiled=True)
        head_rows = jnp.take(gathered.reshape(scen_rows, -1, block_rows), head_index, axis=1)
        pull_summed = jnp.einsum(
            "sjn,jmn->sjm", head_rows, head_blocks, preferred_element_type=jnp.float32
        )
        for touched in range(touches):
            local_rows = jnp.einsum(
                "sbn,jb->sjn", dual_grid, local_half[:, touched], preferred_element_type=jnp.float32
            ).astype(jnp.bfloat16)
            pull_summed = pull_summed + jnp.einsum(
                "sjn,jmn->sjm",
                local_rows,
                local_blocks[:, touched],
                preferred_element_type=jnp.float32,
            )
        pulled = pull_summed.reshape(scen_rows, arc_blks * block_rows)
        risk_mine = risk_now
        mean_risk = lax.psum(jnp.sum(risk_now), "scen") / scen_total
        flows_new = jnp.maximum(
            flow_now - primal_step * (risk_mine[:, None] * arc_costs[None, :] - pulled), 0.0
        )
        level_new = level - primal_step * (1.0 - mean_risk)
        flows_bar = 2.0 * flows_new - flow_now
        level_bar = 2.0 * level_new - level
        partial_value = jnp.sum(arc_costs[None, :] * flows_bar, axis=1) / arc_total
        excess_new = jnp.maximum(excess_now - primal_step * (tail_weight - risk_now), 0.0)
        excess_bar = 2.0 * excess_new - excess_now
        losses = lax.psum(partial_value, "net")
        risk_now = jnp.maximum(risk_now + risk_step * (losses - excess_bar - level_bar), 0.0)
        excess_now = excess_new
        flow_grid = flows_bar.astype(jnp.bfloat16).reshape(scen_rows, arc_blks, block_rows)
        own_terms = jnp.einsum(
            "sjm,jmn->sjn", flow_grid, head_blocks, preferred_element_type=jnp.float32
        )
        term_pack = jnp.where(
            slot_filled[None, :, None], jnp.take(own_terms, slot_source, axis=1), 0.0
        )
        arrived = lax.all_to_all(
            term_pack.reshape(scen_rows, net_size, slot_cap, block_rows),
            "net",
            split_axis=1,
            concat_axis=1,
            tiled=True,
        )
        head_terms = arrived.reshape(scen_rows, slot_count, block_rows)
        summed = jnp.einsum("sqn,qb->sbn", head_terms, asked_wide, precision=select_prec)
        local_terms = jnp.einsum(
            "sjm,jkmn->sjkn", flow_grid, local_blocks, preferred_element_type=jnp.float32
        )
        summed = summed + jnp.einsum(
            "sjkn,jkb->sbn", local_terms, local_wide, precision=select_prec
        )
        dual_now = dual_now + dual_step * (
            demand - summed.reshape(scen_rows, node_blks * block_rows)
        )
        flow_now = flows_new
        level = level_new
    return (flow_now, dual_now, excess_now, risk_now, level)


def solution(mesh):
    placed = (
        P("scen", "net"),
        P("scen", "net"),
        P("scen", "net"),
        P("scen"),
        P("scen"),
        P(),
        P("net"),
        P("net", None, None, None),
        P("net", None, None),
        P("net", None),
        P("net"),
    )
    return jax.shard_map(
        per_device,
        mesh=mesh,
        in_specs=placed,
        out_specs=(P("scen", "net"), P("scen", "net"), P("scen"), P("scen"), P()),
        check_vma=False,
    )
```

profile of v0, /device:TPU:0, one launch (start us, length us, event | category | flops | bytes accessed | tf_op | source)
XLA Modules:
  0.0 597.3 jit_solution(4962526115088580452)
XLA Ops:
  10.9 9.6 %all-to-all-start = ((s32[32,1,4]{2,1,0:T(1,128)}), s32[32,1,4]{2,1,0:T(1,128)S(1)}, u32[]{:S(2)}, u32[]{:S(2)}) async-start(s32[32,1,4]{2,1,0:T(1,128)} %bitcast.20), calls=%async_computation | async-start | bytes 32768 | tf_op jit(solution)/shard_map/all_to_all | solution.py:52
  27.9 3.8 fusion.16
  31.7 3.9 fusion.22
  35.6 58.6 %all-gather.4.cloned.1.call-done = bf16[32,65536]{1,0:T(8,128)(2,1)} async-done(((bf16[32,2048]{1,0:T(8,128)(2,1)}), bf16[32,65536]{1,0:T(8,128)(2,1)}) %all-gather.4.cloned.1.call-update) | async-done | bytes 4194320 | tf_op jit(solution)/shard_map/all_gather | solution.py:66
  94.2 4.9 copy_bitcast_fusion.2
  99.1 3.6 gather_fusion
  116.7 5.4 all-to-all-start.1
  125.6 4.8 convolution_bitcast_fusion.2
  133.5 36.8 %all-to-all-done.1 = f32[32,32,4,128]{3,0,2,1:T(8,128)} async-done(((f32[32,32,4,128]{3,0,2,1:T(8,128)}), f32[32,32,4,128]{3,0,2,1:T(8,128)}, u32[]{:S(2)}, u32[]{:S(2)}) %all-to-all-start.1) | async-done | bytes 2097184 | tf_op jit(solution)/shard_map/all_to_all | solution.py:103
  175.8 13.0 %psum.43 = f32[]{:T(128)} all-reduce(f32[]{:T(128)} %reduce_sum.64), channel_id=1, replica_groups=mesh['net'=32,'scen'=8] {'scen'}, use_global_device_ids=true, to_apply=%region_3.5 | all-reduce | flops 1 | bytes 8 | tf_op jit(solution)/shard_map/psum | solution.py:83
  190.2 72.1 %psum.42 = f32[32]{0:T(128)S(1)} all-reduce(f32[32]{0:T(128)S(1)} %broadcast_multiply_fusion.2), channel_id=1, replica_groups=mesh['net'=32,'scen'=8] {'net'}, use_global_device_ids=true, to_apply=%region_1.3 | all-reduce | flops 32 | bytes 256 | tf_op jit(solution)/shard_map/psum | solution.py:93
  268.9 3.9 fusion.14
  272.8 3.8 fusion.20
  276.5 4.9 copy_bitcast_fusion.1
  281.4 3.6 gather_fusion.2
  292.7 3.2 gather_fusion.3
  299.0 4.8 all-to-all-start.2
  305.5 4.8 convolution_bitcast_fusion.1
  310.3 3.8 fusion.102
  314.1 26.1 %all-to-all-done.2 = f32[32,32,4,128]{3,0,2,1:T(8,128)} async-done(((f32[32,32,4,128]{3,0,2,1:T(8,128)}), f32[32,32,4,128]{3,0,2,1:T(8,128)}, u32[]{:S(2)}, u32[]{:S(2)}) %all-to-all-start.2) | async-done | bytes 2097184 | tf_op jit(solution)/shard_map/all_to_all | solution.py:103
  345.3 13.1 %psum.45 = f32[]{:T(128)} all-reduce(f32[]{:T(128)} %get-tuple-element.16), channel_id=1, replica_groups=mesh['net'=32,'scen'=8] {'scen'}, use_global_device_ids=true, to_apply=%region_11.14 | all-reduce | flops 1 | bytes 8 | tf_op jit(solution)/shard_map/psum | solution.py:83
  359.1 74.1 %psum.44 = f32[32]{0:T(128)S(1)} all-reduce(f32[32]{0:T(128)S(1)} %broadcast_multiply_fusion.1), channel_id=1, replica_groups=mesh['net'=32,'scen'=8] {'net'}, use_global_device_ids=true, to_apply=%region_9.12 | all-reduce | flops 32 | bytes 256 | tf_op jit(solution)/shard_map/psum | solution.py:93
  436.9 3.8 fusion.6
  440.7 3.9 fusion.12
  444.6 3.8 fusion.18
  448.4 4.9 copy_bitcast_fusion
  453.3 3.6 gather_fusion.4
  465.4 3.2 gather_fusion.5
  471.7 4.8 all-to-all-start.3
  476.4 13.9 %psum.47 = f32[]{:T(128)} all-reduce(f32[]{:T(128)} %get-tuple-element.11), channel_id=1, replica_groups=mesh['net'=32,'scen'=8] {'scen'}, use_global_device_ids=true, to_apply=%region_15.18 | all-reduce | flops 1 | bytes 8 | tf_op jit(solution)/shard_map/psum | solution.py:83
  492.4 83.1 %psum.46 = f32[32]{0:T(128)S(1)} all-reduce(f32[32]{0:T(128)S(1)} %broadcast_multiply_fusion), channel_id=1, replica_groups=mesh['net'=32,'scen'=8] {'net'}, use_global_device_ids=true, to_apply=%region_13.16 | all-reduce | flops 32 | bytes 256 | tf_op jit(solution)/shard_map/psum | solution.py:93
  576.1 4.8 convolution_bitcast_fusion
  (143 shorter events, 86.3 us)
Async XLA Ops:
  7.2 95.6 %copy-start = (bf16[64,128,128]{2,1,0:T(8,128)(2,1)S(1)}, bf16[64,128,128]{2,1,0:T(8,128)(2,1)}, u32[]{:S(2)}) copy-start(bf16[64,128,128]{2,1,0:T(8,128)(2,1)} %param.23) | copy-start | bytes 6291460
  7.2 87.1 %all-gather.4.cloned.1.call-start = ((), (), s32[]{:S(2)}) async-start(), calls=%async_computation.4 | async-start | bytes 4325376 | tf_op jit(solution)/shard_map/all_gather | solution.py:66
  10.9 105.9 %all-to-all-start = ((s32[32,1,4]{2,1,0:T(1,128)}), s32[32,1,4]{2,1,0:T(1,128)S(1)}, u32[]{:S(2)}, u32[]{:S(2)}) async-start(s32[32,1,4]{2,1,0:T(1,128)} %bitcast.20), calls=%async_computation | async-start | bytes 32768 | tf_op jit(solution)/shard_map/all_to_all | solution.py:52
  102.7 2.4 copy-start.9
  102.7 2.4 copy-start.11
  102.7 2.5 copy-start.22
  105.2 3.0 copy-start.3
  105.2 3.0 copy-start.25
  105.2 3.0 copy-start.27
  108.8 15.3 %copy-start.1 = (f32[32,8192]{1,0:T(8,128)}, f32[32,8192]{1,0:T(8,128)S(1)}, u32[]{:S(2)}) copy-start(f32[32,8192]{1,0:T(8,128)S(1)} %get-tuple-element.21) | copy-start | bytes 3145732
  116.7 53.5 %all-to-all-start.1 = ((f32[32,32,4,128]{3,0,2,1:T(8,128)}), f32[32,32,4,128]{3,0,2,1:T(8,128)}, u32[]{:S(2)}, u32[]{:S(2)}) async-start(f32[32,32,4,128]{3,0,2,1:T(8,128)} %bitcast.330), calls=%async_computation.1 | async-start | bytes 4194304 | tf_op jit(solution)/shard_map/all_to_all | solution.py:103
  122.2 154.4 %all-gather.6.cloned.1.call-start = ((), (), s32[]{:S(2)}) async-start(), calls=%async_computation.5 | async-start | bytes 4325376 | tf_op jit(solution)/shard_map/all_gather | solution.py:66
  125.5 4.9 copy-start.26
  173.2 1.2 copy-start.5
  173.2 1.2 copy-start.16
  173.2 89.1 %copy-start.28 = (f32[32]{0:T(128)S(1)}, f32[32]{0:T(128)}, u32[]{:S(2)}) copy-start(f32[32]{0:T(128)} %param.18) | copy-start | bytes 388
  285.0 2.4 copy-start.10
  285.0 2.4 copy-start.12
  285.0 2.4 copy-start.23
  287.5 3.0 copy-start.2
  299.0 41.3 %all-to-all-start.2 = ((f32[32,32,4,128]{3,0,2,1:T(8,128)}), f32[32,32,4,128]{3,0,2,1:T(8,128)}, u32[]{:S(2)}, u32[]{:S(2)}) async-start(f32[32,32,4,128]{3,0,2,1:T(8,128)} %bitcast.331), calls=%async_computation.2 | async-start | bytes 4194304 | tf_op jit(solution)/shard_map/all_to_all | solution.py:103
  303.8 144.6 %all-gather.8.cloned.1.call-start = ((), (), s32[]{:S(2)}) async-start(), calls=%async_computation.6 | async-start | bytes 4325376 | tf_op jit(solution)/shard_map/all_gather | solution.py:66
  340.3 3.0 copy-start.24
  343.2 1.2 copy-start.14
  343.3 1.2 copy-start.17
  456.9 2.4 copy-start.6
  456.9 2.4 copy-start.7
  456.9 2.5 copy-start.8
  456.9 2.5 copy-start.21
  471.7 112.4 %all-to-all-start.3 = ((f32[32,32,4,128]{3,0,2,1:T(8,128)}), f32[32,32,4,128]{3,0,2,1:T(8,128)}, u32[]{:S(2)}, u32[]{:S(2)}) async-start(f32[32,32,4,128]{3,0,2,1:T(8,128)} %bitcast.329), calls=%async_computation.3 | async-start | bytes 4194304 | tf_op jit(solution)/shard_map/all_to_all | solution.py:103
  587.0 1.0 copy-start.18
  587.0 1.1 copy-start.20
  (4 other events, 3.3 us)
Sparse Core Ops, SparseCore 0:
  11.2 83.0 all-gather.3
  175.4 78.8 all-gather.5
  345.4 77.5 all-gather.7
where the time goes:
time: 606 us; the launch traced here: 597 us
  blocking collectives  269 us (44%)
  waiting for transfers between devices  122 us (20%)
  matrix products  85.9 us (14%)
  local copies, waits for them, and re-layouts  50.6 us (8%)
  other arithmetic  25.8 us (4%)
  starting transfers between devices  25.4 us (4%)
  between operations  18.5 us (3%)
    psum x3, blocking collectives, per_device(): losses = lax.psum(partial_value, 'net')  229 us
    all_to_all x3, waiting for transfers between devices, per_device(): lax.all_to_all(term_pack.reshape(scen_rows, net_size, slot_cap, block_row...  62.9 us
    all_gather x3, waiting for transfers between devices, per_device(): gathered = lax.all_gather(dual_panel, 'net', axis=1, tiled=True)  58.6 us
    dot_general x12, matrix products, per_device(): jnp.einsum('sjn,jmn->sjm', local_rows, local_blocks[:, touched], preferre...  41.3 us
    psum x3, blocking collectives, per_device(): mean_risk = lax.psum(jnp.sum(risk_now), 'scen') / scen_total  40 us
    all_to_all x3, starting transfers between devices, per_device(): lax.all_to_all(term_pack.reshape(scen_rows, net_size, slot_cap, block_row...  15 us
    reshape x3, local copies, waits for them, and re-layouts, per_device(): gathered.reshape(scen_rows, -1, block_rows)  14.6 us
    dot_general x3, matrix products, per_device(): jnp.einsum('sjm,jkmn->sjkn', flow_grid, local_blocks, preferred_element_t...  14.5 us
  transfers between devices with their start and end apart: 7, of which 3 were waited for; matrix products, arithmetic and copies ran while one was open for 17% of the time, Pallas kernels for 0%

commit v1 on v0

--- a/solution.py
+++ b/solution.py
@@ -8,6 +8,13 @@
 dual_step = 0.5
 risk_step = 1.0
 tail_weight = 2.0
+
+
+def swapped_in(shard, mesh_axis, dim):
+    size = lax.axis_size(mesh_axis)
+    blocks = jnp.stack([shard for _ in range(size)])
+    blocks = lax.all_to_all(blocks, mesh_axis, split_axis=0, concat_axis=0)
+    return jnp.concatenate(blocks, axis=dim)
 
 
 def per_device(
@@ -63,7 +70,7 @@
     for iteration in range(ROUNDS):
         dual_panel = dual_now.astype(jnp.bfloat16)
         dual_grid = dual_panel.reshape(scen_rows, node_blks, block_rows)
-        gathered = lax.all_gather(dual_panel, "net", axis=1, tiled=True)
+        gathered = swapped_in(dual_panel, "net", 1)
         head_rows = jnp.take(gathered.reshape(scen_rows, -1, block_rows), head_index, axis=1)
         pull_summed = jnp.einsum(
             "sjn,jmn->sjm", head_rows, head_blocks, preferred_element_type=jnp.float32

time: 606 us -> 811 us (1.34)
  blocking collectives: 269 us -> 387 us
  local copies, waits for them, and re-layouts: 50.6 us -> 104 us
  waiting for transfers between devices: 122 us -> 148 us
  starting transfers between devices: 25.4 us -> 47.7 us
  between operations: 18.5 us -> 5.33 us
    psum x3, blocking collectives: 229 us -> 345 us  [per_device(): losses = lax.psum(partial_value, 'net')]
    all_to_all x0 -> x3, waiting for transfers between devices: none -> 82.9 us  [swapped_in(): blocks = lax.all_to_all(blocks, mesh_axis, split_axis=0, concat_axis=0)]
    all_gather x3 -> x0, waiting for transfers between devices: 58.6 us -> none  [per_device(): gathered = lax.all_gather(dual_panel, 'net', axis=1, tiled=True)]
    another operation x0 -> x9, local copies, waits for them, and re-layouts: none -> 50.2 us  [the longest x6 42.7 us: per_device(): gathered.reshape(scen_rows, -1, block_rows)]
    all_to_all x0 -> x3, starting transfers between devices: none -> 22.8 us  [swapped_in(): blocks = lax.all_to_all(blocks, mesh_axis, split_axis=0, concat_axis=0)]
  transfers between devices with their start and end apart: 7 -> 7, of which waited for: 3 -> 3; matrix products, arithmetic and copies ran while one was open for 17% -> 14% of each run, Pallas kernels for 0% -> 0%
where the time goes in v1:
time: 811 us; the launch traced here: 803 us
  blocking collectives  387 us (48%)
  waiting for transfers between devices  148 us (18%)
  local copies, waits for them, and re-layouts  104 us (13%)
  matrix products  86 us (11%)
  starting transfers between devices  47.7 us (6%)
  other arithmetic  24.4 us (3%)
    psum x3, blocking collectives, per_device(): losses = lax.psum(partial_value, 'net')  345 us
    all_to_all x3, waiting for transfers between devices, swapped_in(): blocks = lax.all_to_all(blocks, mesh_axis, split_axis=0, concat_axis=0)  82.9 us
    all_to_all x3, waiting for transfers between devices, per_device(): lax.all_to_all(term_pack.reshape(scen_rows, net_size, slot_cap, block_row...  65.3 us
    another operation x6, local copies, waits for them, and re-layouts, per_device(): gathered.reshape(scen_rows, -1, block_rows)  42.7 us
    psum x3, blocking collectives, per_device(): mean_risk = lax.psum(jnp.sum(risk_now), 'scen') / scen_total  42.3 us
    dot_general x12, matrix products, per_device(): jnp.einsum('sjn,jmn->sjm', local_rows, local_blocks[:, touched], preferre...  41.4 us
    all_to_all x3, starting transfers between devices, swapped_in(): blocks = lax.all_to_all(blocks, mesh_axis, split_axis=0, concat_axis=0)  22.8 us
    all_to_all x3, starting transfers between devices, per_device(): lax.all_to_all(term_pack.reshape(scen_rows, net_size, slot_cap, block_row...  19.8 us
  transfers between devices with their start and end apart: 7, of which 3 were waited for; matrix products, arithmetic and copies ran while one was open for 14% of the time, Pallas kernels for 0%

profile of v1, /device:TPU:0, one launch (start us, length us, event | category | flops | bytes accessed | tf_op | source)
XLA Modules:
  0.0 802.6 jit_solution(3090485199507391193)
XLA Ops:
  4.3 9.9 %all-to-all-start = ((bf16[32,32,2048]{2,1,0:T(8,128)(2,1)}), bf16[32,32,2048]{2,1,0:T(8,128)(2,1)}, u32[]{:S(2)}, u32[]{:S(2)}) async-start(bf16[32,32,2048]{2,1,0:T(8,128)(2,1)} %stack.6), calls=%async_computation | async-start | bytes 8388608 | tf_op jit(solution)/shard_map/all_to_all | solution.py:16
  20.5 3.8 fusion.16
  24.4 3.9 fusion.22
  28.3 82.9 %all-to-all-done = bf16[32,32,2048]{2,1,0:T(8,128)(2,1)} async-done(((bf16[32,32,2048]{2,1,0:T(8,128)(2,1)}), bf16[32,32,2048]{2,1,0:T(8,128)(2,1)}, u32[]{:S(2)}, u32[]{:S(2)}) %all-to-all-start) | async-done | bytes 4194336 | tf_op jit(solution)/shard_map/all_to_all | solution.py:16
  111.1 5.1 all-to-all-start.1
  116.3 6.5 copy.80
  122.7 7.4 reshape_reshape.9
  130.1 6.9 copy.81
  154.6 10.2 %all-to-all-start.2 = ((f32[32,32,4,128]{3,0,2,1:T(8,128)}), f32[32,32,4,128]{3,0,2,1:T(8,128)}, u32[]{:S(2)}, u32[]{:S(2)}) async-start(f32[32,32,4,128]{3,0,2,1:T(8,128)} %bitcast.318), calls=%async_computation.2 | async-start | bytes 4194304 | tf_op jit(solution)/shard_map/all_to_all | solution.py:110
  167.7 4.8 convolution_bitcast_fusion.2
  175.6 38.8 %all-to-all-done.2 = f32[32,32,4,128]{3,0,2,1:T(8,128)} async-done(((f32[32,32,4,128]{3,0,2,1:T(8,128)}), f32[32,32,4,128]{3,0,2,1:T(8,128)}, u32[]{:S(2)}, u32[]{:S(2)}) %all-to-all-start.2) | async-done | bytes 2097184 | tf_op jit(solution)/shard_map/all_to_all | solution.py:110
  221.2 6.2 all-to-all-start.3
  228.0 15.5 %psum.43 = f32[]{:T(128)} all-reduce(f32[]{:T(128)} %reduce_sum.64), channel_id=1, replica_groups=mesh['net'=32,'scen'=8] {'scen'}, use_global_device_ids=true, to_apply=%region_3.5 | all-reduce | flops 1 | bytes 8 | tf_op jit(solution)/shard_map/psum | solution.py:90
  244.8 138.9 %psum.42 = f32[32]{0:T(128)S(1)} all-reduce(f32[32]{0:T(128)S(1)} %broadcast_multiply_fusion.2), channel_id=1, replica_groups=mesh['net'=32,'scen'=8] {'net'}, use_global_device_ids=true, to_apply=%region_1.3 | all-reduce | flops 32 | bytes 256 | tf_op jit(solution)/shard_map/psum | solution.py:100
  393.2 3.9 fusion.8
  397.1 6.5 copy.96
  403.5 7.4 reshape_reshape.10
  410.9 6.9 copy.97
  436.1 4.8 all-to-all-start.4
  442.3 4.8 convolution_bitcast_fusion.1
  451.0 26.5 %all-to-all-done.4 = f32[32,32,4,128]{3,0,2,1:T(8,128)} async-done(((f32[32,32,4,128]{3,0,2,1:T(8,128)}), f32[32,32,4,128]{3,0,2,1:T(8,128)}, u32[]{:S(2)}, u32[]{:S(2)}) %all-to-all-start.4) | async-done | bytes 2097184 | tf_op jit(solution)/shard_map/all_to_all | solution.py:110
  484.4 6.7 all-to-all-start.5
  491.1 13.5 %psum.45 = f32[]{:T(128)} all-reduce(f32[]{:T(128)} %get-tuple-element.16), channel_id=1, replica_groups=mesh['net'=32,'scen'=8] {'scen'}, use_global_device_ids=true, to_apply=%region_11.14 | all-reduce | flops 1 | bytes 8 | tf_op jit(solution)/shard_map/psum | solution.py:90
  506.4 129.7 %psum.44 = f32[32]{0:T(128)} all-reduce(f32[32]{0:T(128)} %broadcast_multiply_fusion.1), channel_id=1, replica_groups=mesh['net'=32,'scen'=8] {'net'}, use_global_device_ids=true, to_apply=%region_9.12 | all-reduce | flops 32 | bytes 256 | tf_op jit(solution)/shard_map/psum | solution.py:100
  640.2 3.9 fusion.12
  651.7 6.5 copy.107
  658.2 7.4 reshape_reshape.11
  665.6 6.8 copy.108
  691.4 4.8 all-to-all-start.6
  696.2 13.3 %psum.47 = f32[]{:T(128)} all-reduce(f32[]{:T(128)} %get-tuple-element.11), channel_id=1, replica_groups=mesh['net'=32,'scen'=8] {'scen'}, use_global_device_ids=true, to_apply=%region_15.18 | all-reduce | flops 1 | bytes 8 | tf_op jit(solution)/shard_map/psum | solution.py:90
  711.7 76.0 %psum.46 = f32[32]{0:T(128)S(1)} all-reduce(f32[32]{0:T(128)S(1)} %broadcast_multiply_fusion), channel_id=1, replica_groups=mesh['net'=32,'scen'=8] {'net'}, use_global_device_ids=true, to_apply=%region_13.16 | all-reduce | flops 32 | bytes 256 | tf_op jit(solution)/shard_map/psum | solution.py:100
  788.2 4.8 convolution_bitcast_fusion
  (175 shorter events, 122.4 us)
Async XLA Ops:
  0.6 140.0 %copy-start = (bf16[64,128,128]{2,1,0:T(8,128)(2,1)S(1)}, bf16[64,128,128]{2,1,0:T(8,128)(2,1)}, u32[]{:S(2)}) copy-start(bf16[64,128,128]{2,1,0:T(8,128)(2,1)} %param.23) | copy-start | bytes 6291460
  4.3 9.9 %copy-start.5 = (f32[32,2048]{1,0:T(8,128)S(1)}, f32[32,2048]{1,0:T(8,128)}, u32[]{:S(2)}) copy-start(f32[32,2048]{1,0:T(8,128)} %param.16) | copy-start | bytes 786436
  4.3 10.0 %copy-start.41 = (s32[64]{0:T(128)S(1)}, s32[64]{0:T(128)}, u32[]{:S(2)}) copy-start(s32[64]{0:T(128)} %param.25) | copy-start | bytes 772
  4.3 11.2 %copy-start.27 = (s32[64,4]{0,1:T(4,128)S(1)}, s32[64,4]{0,1:T(4,128)}, u32[]{:S(2)}) copy-start(s32[64,4]{0,1:T(4,128)} %param.24) | copy-start | bytes 3076
  4.3 106.9 %all-to-all-start = ((bf16[32,32,2048]{2,1,0:T(8,128)(2,1)}), bf16[32,32,2048]{2,1,0:T(8,128)(2,1)}, u32[]{:S(2)}, u32[]{:S(2)}) async-start(bf16[32,32,2048]{2,1,0:T(8,128)(2,1)} %stack.6), calls=%async_computation | async-start | bytes 8388608 | tf_op jit(solution)/shard_map/all_to_all | solution.py:16
  15.4 402.3 %copy-start.29 = (s32[1024]{0:T(1024)}, s32[1024]{0:T(1024)S(1)}, u32[]{:S(2)}) copy-start(s32[1024]{0:T(1024)S(1)} %pad_clamp_fusion.1) | copy-start | bytes 12292
  15.5 414.2 %copy-start.28 = (s32[1024]{0:T(1024)}, s32[1024]{0:T(1024)S(1)}, u32[]{:S(2)}) copy-start(s32[1024]{0:T(1024)S(1)} %pad_clamp_fusion) | copy-start | bytes 12292
  15.5 405.9 %copy-start.37 = (pred[64]{0:T(512)(128)(4,1)}, pred[64]{0:T(512)(128)(4,1)S(1)}, u32[]{:S(2)}) copy-start(pred[64]{0:T(512)(128)(4,1)S(1)} %compare_and_fusion) | copy-start | bytes 196
  15.5 417.3 %copy-start.30 = (pred[128]{0:T(512)(128)(4,1)}, pred[128]{0:T(512)(128)(4,1)S(1)}, u32[]{:S(2)}) copy-start(pred[128]{0:T(512)(128)(4,1)S(1)} %get-tuple-element.22) | copy-start | bytes 388
  15.5 417.3 %copy-start.32 = (pred[128]{0:T(512)(128)(4,1)}, pred[128]{0:T(512)(128)(4,1)S(1)}, u32[]{:S(2)}) copy-start(pred[128]{0:T(512)(128)(4,1)S(1)} %get-tuple-element.23) | copy-start | bytes 388
  111.1 43.5 %all-to-all-start.1 = ((s32[32,1,4]{2,1,0:T(1,128)}), s32[32,1,4]{2,1,0:T(1,128)S(1)}, u32[]{:S(2)}, u32[]{:S(2)}) async-start(s32[32,1,4]{2,1,0:T(1,128)} %bitcast.21), calls=%async_computation.1 | async-start | bytes 32768 | tf_op jit(solution)/shard_map/all_to_all | solution.py:59
  143.1 3.0 copy-start.3
  143.1 3.0 copy-start.25
  143.1 3.0 copy-start.34
  146.7 19.5 %copy-start.1 = (f32[32,8192]{1,0:T(8,128)}, f32[32,8192]{1,0:T(8,128)S(1)}, u32[]{:S(2)}) copy-start(f32[32,8192]{1,0:T(8,128)S(1)} %get-tuple-element.21) | copy-start | bytes 3145732
  154.6 59.8 %all-to-all-start.2 = ((f32[32,32,4,128]{3,0,2,1:T(8,128)}), f32[32,32,4,128]{3,0,2,1:T(8,128)}, u32[]{:S(2)}, u32[]{:S(2)}) async-start(f32[32,32,4,128]{3,0,2,1:T(8,128)} %bitcast.318), calls=%async_computation.2 | async-start | bytes 4194304 | tf_op jit(solution)/shard_map/all_to_all | solution.py:110
  221.2 162.5 %copy-start.39 = (f32[32]{0:T(128)S(1)}, f32[32]{0:T(128)}, u32[]{:S(2)}) copy-start(f32[32]{0:T(128)} %param.18) | copy-start | bytes 388
  221.2 175.9 %all-to-all-start.3 = ((bf16[32,32,2048]{2,1,0:T(8,128)(2,1)}), bf16[32,32,2048]{2,1,0:T(8,128)(2,1)}, u32[]{:S(2)}, u32[]{:S(2)}) async-start(bf16[32,32,2048]{2,1,0:T(8,128)(2,1)} %stack.7), calls=%async_computation.3 | async-start | bytes 8388608 | tf_op jit(solution)/shard_map/all_to_all | solution.py:16
  384.3 42.5 %copy-start.35 = (f32[32]{0:T(128)}, f32[32]{0:T(128)S(1)}, u32[]{:S(2)}) copy-start(f32[32]{0:T(128)S(1)} %get-tuple-element.17) | copy-start | bytes 388
  423.8 3.0 copy-start.2
  436.1 41.4 %all-to-all-start.4 = ((f32[32,32,4,128]{3,0,2,1:T(8,128)}), f32[32,32,4,128]{3,0,2,1:T(8,128)}, u32[]{:S(2)}, u32[]{:S(2)}) async-start(f32[32,32,4,128]{3,0,2,1:T(8,128)} %bitcast.319), calls=%async_computation.4 | async-start | bytes 4194304 | tf_op jit(solution)/shard_map/all_to_all | solution.py:110
  477.5 3.0 copy-start.24
  484.4 167.3 %all-to-all-start.5 = ((bf16[32,32,2048]{2,1,0:T(8,128)(2,1)}), bf16[32,32,2048]{2,1,0:T(8,128)(2,1)}, u32[]{:S(2)}, u32[]{:S(2)}) async-start(bf16[32,32,2048]{2,1,0:T(8,128)(2,1)} %stack.8), calls=%async_computation.5 | async-start | bytes 8388608 | tf_op jit(solution)/shard_map/all_to_all | solution.py:16
  665.6 10.6 %copy-start.38 = (pred[64]{0:T(512)(128)(4,1)S(1)}, pred[64]{0:T(512)(128)(4,1)}, u32[]{:S(2)}) copy-start(pred[64]{0:T(512)(128)(4,1)} %copy-done.37) | copy-start | bytes 196
  676.1 2.5 copy-start.10
  676.1 2.5 copy-start.22
  678.6 2.9 copy-start.26
  678.6 2.9 copy-start.36
  684.8 3.4 copy-start.31
  684.8 3.4 copy-start.33
  691.4 104.7 %all-to-all-start.6 = ((f32[32,32,4,128]{3,0,2,1:T(8,128)}), f32[32,32,4,128]{3,0,2,1:T(8,128)}, u32[]{:S(2)}, u32[]{:S(2)}) async-start(f32[32,32,4,128]{3,0,2,1:T(8,128)} %bitcast.317), calls=%async_computation.6 | async-start | bytes 4194304 | tf_op jit(solution)/shard_map/all_to_all | solution.py:110
  696.2 91.5 %copy-start.40 = (f32[32]{0:T(128)S(1)}, f32[32]{0:T(128)}, u32[]{:S(2)}) copy-start(f32[32]{0:T(128)} %get-tuple-element.13) | copy-start | bytes 388
  (17 other events, 28.6 us)
